TPU v7x, 32 devices: a whole 2x2x4 slice. The times are simulated.
32 devices in a mesh: fsdp: 4 (over z), rep: 8 (over y, x, core).
Axes of the slice: x: 2, y: 2, z: 4, core: 2. Of those that a mesh axis runs over, the one named last changes fastest.
Arguments:
- tokens: bfloat16 [8, 512, 2048], P('rep', 'fsdp'), may hold values from -6 to 6
- cotangent: bfloat16 [8, 512, 2048], P('rep', 'fsdp'), may hold values from -6 to 6
- lengths: int32 [8, 8], P('rep'), may hold values from 32 to 96, as said below
- deal_order: int32 [8, 8], P('rep'), may hold values from 0 to 7, as said below
- attn_gain: bfloat16 [2048], P('fsdp'), may hold values from 0.099609375 to 1.8984375
- mlp_gain: bfloat16 [2048], P('fsdp'), may hold values from 0.099609375 to 1.8984375
- q_scale: bfloat16 [128], P('fsdp'), may hold values from 0.099609375 to 1.8984375
- k_scale: bfloat16 [128], P('fsdp'), may hold values from 0.099609375 to 1.8984375
- w_qkv: bfloat16 [2048, 4096], P('fsdp'), may hold values from -0.125 to 0.125
- w_hgate: bfloat16 [2048, 16], P('fsdp'), may hold values from -0.125 to 0.125
- w_out: bfloat16 [2048, 2048], P('fsdp'), may hold values from -1.5 to 1.5
- w_gate: bfloat16 [2048, 6144], P('fsdp'), may hold values from -0.125 to 0.125
- w_up: bfloat16 [2048, 6144], P('fsdp'), may hold values from -0.125 to 0.125
- w_down: bfloat16 [2048, 6144], P('fsdp'), may hold values from -0.078125 to 0.078125
Outputs:
- output: bfloat16 [8, 512, 2048], P('rep', 'fsdp')
- tokens_grad: bfloat16 [8, 512, 2048], P('rep', 'fsdp')
- attn_gain_grad: float32 [2048], P('fsdp')
- mlp_gain_grad: float32 [2048], P('fsdp')
- q_scale_grad: float32 [128], P('fsdp')
- k_scale_grad: float32 [128], P('fsdp')
- w_qkv_grad: float32 [2048, 4096], P('fsdp')
- w_hgate_grad: float32 [2048, 16], P('fsdp')
- w_out_grad: float32 [2048, 2048], P('fsdp')
- w_gate_grad: float32 [2048, 6144], P('fsdp')
- w_up_grad: float32 [2048, 6144], P('fsdp')
- w_down_grad: float32 [2048, 6144], P('fsdp')
Inputs may be any that keep to these rules, and one draw needn't show every extreme that they name: `lengths`: every length is a multiple of 32; the 2 sequences dealt to each index of fsdp hold 128 tokens together. `deal_order`: each row is a permutation of the group's sequences.
All inputs are finite; a program needn't handle non-finite values.
Results may differ from a plain program's by a relative error of at most 0.015.
Values may be sent and summed in bfloat16 or wider, within the bound.
A program may use at most 704 MiB of HBM per device.

v0:
```python
import jax
import jax.numpy as jnp
from jax import lax
from jax.sharding import PartitionSpec as P

QUERY_HEADS = 16
KEY_VALUE_HEADS = 8
HEAD_SIZE = 128
FF = 6144


eps_norm = 1e-06
rope_base = 1000000.0


def matmul(left, right):
    return jnp.dot(left, right, preferred_element_type=jnp.float32)


def contract_rows(left, right):
    return lax.dot_general(
        left, right, (((0,), (0,)), ((), ())), preferred_element_type=jnp.float32
    )


def contract_cols(left, right):
    return lax.dot_general(
        left, right, (((1,), (1,)), ((), ())), preferred_element_type=jnp.float32
    )


def exclusive(value_rows):
    return jnp.cumsum(value_rows) - value_rows


def lookup(indices, entries):
    onehot = (indices[:, None] == jnp.arange(entries.shape[0], dtype=jnp.int32)[None, :]).astype(
        jnp.int32
    )
    return jnp.sum(onehot * entries[None, :], axis=1)


def normalize(value_rows):
    factor = lax.rsqrt(jnp.mean(value_rows * value_rows, axis=-1, keepdims=True) + eps_norm)
    return (value_rows * factor, factor)


def norm_back(grad_normed, normed_unit, factor, gain):
    scaled = grad_normed * gain
    return factor * (scaled - normed_unit * jnp.mean(scaled * normed_unit, axis=-1, keepdims=True))


def rope_tables(positions):
    half_dim = HEAD_SIZE // 2
    frequency = jnp.power(rope_base, -2.0 * jnp.arange(half_dim, dtype=jnp.float32) / HEAD_SIZE)
    angles = positions.astype(jnp.float32)[:, None] * frequency[None, :]
    angles = jnp.concatenate([angles, angles], axis=1)
    return (jnp.cos(angles)[:, None, :], jnp.sin(angles)[:, None, :])


def rotate(value_rows, cosine, sine_table):
    half_dim = value_rows.shape[-1] // 2
    turned = jnp.concatenate([-value_rows[..., half_dim:], value_rows[..., :half_dim]], axis=-1)
    return value_rows * cosine + turned * sine_table


def unrotate(grads, cosine, sine_table):
    half_dim = grads.shape[-1] // 2
    shifted = grads * sine_table
    turned = jnp.concatenate([shifted[..., half_dim:], -shifted[..., :half_dim]], axis=-1)
    return grads * cosine + turned


def attention_scores(queries, keys_rot, allowed):
    scores = jnp.einsum(
        "qkgd,pkd->kgqp", queries, keys_rot, preferred_element_type=jnp.float32
    ) * HEAD_SIZE ** (-0.5)
    return jnp.where(allowed[None, None], scores, -1e30)


def pick_rows(wanted, carried, pieces):
    count_of_rows = pieces[0].shape[-2]
    inside = ((wanted >= 0) & (wanted < count_of_rows))[:, None]
    position_in = jnp.clip(wanted, 0, count_of_rows - 1)
    return tuple(
        (
            jnp.where(
                inside,
                jnp.take(
                    shard_piece.reshape(count_of_rows, shard_piece.shape[-1]), position_in, axis=0
                ),
                previous,
            )
            for shard_piece, previous in zip(pieces, carried)
        )
    )


def on_device(
    tokens,
    cotangent,
    lengths,
    deal_order,
    attn_gain,
    mlp_gain,
    q_scale,
    k_scale,
    w_qkv,
    w_hgate,
    w_out,
    w_gate,
    w_up,
    w_down,
):
    count_of_rows = tokens.shape[1]
    width = tokens.shape[2]
    devices_fsdp = lax.axis_size("fsdp")
    shard = lax.axis_index("fsdp")
    seq_lengths = lengths[0]
    seq_order = deal_order[0]
    seq_count = seq_lengths.shape[0]
    seq_index = jnp.arange(seq_count, dtype=jnp.int32)
    starts = exclusive(seq_lengths)
    chosen = (seq_order[:, None] == seq_index[None, :]).astype(jnp.int32)
    dealt_lengths = jnp.sum(chosen * seq_lengths[None, :], axis=1)
    dealt_sources = jnp.sum(chosen * starts[None, :], axis=1)
    dealt_starts = exclusive(dealt_lengths)
    local_rows = jnp.arange(count_of_rows, dtype=jnp.int32)
    global_rows = shard * count_of_rows + local_rows
    segment = jnp.sum((global_rows[:, None] >= dealt_starts[None, 1:]).astype(jnp.int32), axis=1)
    position = global_rows - lookup(segment, dealt_starts)
    source = lookup(segment, dealt_sources) + position
    home_seq = jnp.sum((global_rows[:, None] >= starts[None, 1:]).astype(jnp.int32), axis=1)
    slot_of = jnp.sum(chosen * seq_index[:, None], axis=0)
    target = (
        lookup(lookup(home_seq, slot_of), dealt_starts) + global_rows - lookup(home_seq, starts)
    )
    blank = jnp.zeros((count_of_rows, width), jnp.bfloat16)
    dealt_in, dealt_cot = pick_rows(
        source,
        (blank, blank),
        (
            lax.all_gather(tokens, "fsdp", axis=1, tiled=True),
            lax.all_gather(cotangent, "fsdp", axis=1, tiled=True),
        ),
    )
    attn_parts = (
        lax.all_gather(attn_gain, "fsdp", axis=0, tiled=True),
        lax.all_gather(mlp_gain, "fsdp", axis=0, tiled=True),
        lax.all_gather(q_scale, "fsdp", axis=0, tiled=True),
        lax.all_gather(k_scale, "fsdp", axis=0, tiled=True),
        lax.all_gather(w_qkv, "fsdp", axis=0, tiled=True),
        lax.all_gather(w_hgate, "fsdp", axis=0, tiled=True),
        lax.all_gather(w_out, "fsdp", axis=0, tiled=True),
    )
    gain_one = attn_parts[0].astype(jnp.float32)
    gain_two = attn_parts[1].astype(jnp.float32)
    query_gain = attn_parts[2].astype(jnp.float32)
    key_gain = attn_parts[3].astype(jnp.float32)
    stream = dealt_in.astype(jnp.float32)
    unit_one, factor_one = normalize(stream)
    normed_one = (unit_one * gain_one).astype(jnp.bfloat16)
    projected_rows = matmul(normed_one, attn_parts[4])
    head_logit = matmul(normed_one, attn_parts[5])
    group_list = QUERY_HEADS // KEY_VALUE_HEADS
    query_raw = projected_rows[:, : QUERY_HEADS * HEAD_SIZE].reshape(
        count_of_rows, QUERY_HEADS, HEAD_SIZE
    )
    key_unrotated = projected_rows[
        :, QUERY_HEADS * HEAD_SIZE : (QUERY_HEADS + KEY_VALUE_HEADS) * HEAD_SIZE
    ].reshape(count_of_rows, KEY_VALUE_HEADS, HEAD_SIZE)
    value_rows = (
        projected_rows[:, (QUERY_HEADS + KEY_VALUE_HEADS) * HEAD_SIZE :]
        .reshape(count_of_rows, KEY_VALUE_HEADS, HEAD_SIZE)
        .astype(jnp.bfloat16)
    )
    query_unit, query_factor = normalize(query_raw)
    key_unit, key_factor = normalize(key_unrotated)
    cosine, sine_table = rope_tables(position)
    queries = (
        rotate(query_unit * query_gain, cosine, sine_table)
        .astype(jnp.bfloat16)
        .reshape(count_of_rows, KEY_VALUE_HEADS, group_list, HEAD_SIZE)
    )
    keys_rot = rotate(key_unit * key_gain, cosine, sine_table).astype(jnp.bfloat16)
    allowed = (segment[:, None] == segment[None, :]) & (local_rows[None, :] <= local_rows[:, None])
    scores = attention_scores(queries, keys_rot, allowed)
    row_max = jnp.max(scores, axis=-1, keepdims=True)
    weights_exp = jnp.exp(scores - row_max)
    row_total = jnp.sum(weights_exp, axis=-1, keepdims=True)
    probabilities = weights_exp / row_total
    log_total = row_max + jnp.log(row_total)
    head_out = jnp.einsum(
        "kgqp,pkd->qkgd",
        probabilities.astype(jnp.bfloat16),
        value_rows,
        preferred_element_type=jnp.float32,
    ).reshape(count_of_rows, QUERY_HEADS, HEAD_SIZE)
    head_gate = jax.nn.sigmoid(head_logit)
    gated = (
        (head_out * head_gate[:, :, None])
        .astype(jnp.bfloat16)
        .reshape(count_of_rows, QUERY_HEADS * HEAD_SIZE)
    )
    residual = stream + contract_cols(gated, attn_parts[6])
    unit_two, factor_two = normalize(residual)
    normed_two = (unit_two * gain_two).astype(jnp.bfloat16)
    mlp_parts = (
        lax.all_gather(w_gate, "fsdp", axis=0, tiled=True),
        lax.all_gather(w_up, "fsdp", axis=0, tiled=True),
        lax.all_gather(w_down, "fsdp", axis=0, tiled=True),
    )
    gate_pre = matmul(normed_two, mlp_parts[0])
    up_pre = matmul(normed_two, mlp_parts[1])
    gate_sig = jax.nn.sigmoid(gate_pre)
    gate_act = gate_pre * gate_sig
    hidden = (gate_act * up_pre).astype(jnp.bfloat16)
    final_rows = (residual + contract_cols(hidden, mlp_parts[2])).astype(jnp.bfloat16)
    grad_out = dealt_cot.astype(jnp.float32)
    cot_cols = dealt_cot
    grad_hidden = matmul(cot_cols, lax.all_gather(w_down, "fsdp", axis=0, tiled=True))
    grad_gate = (grad_hidden * up_pre * gate_sig * (1.0 + gate_pre * (1.0 - gate_sig))).astype(
        jnp.bfloat16
    )
    grad_up = (grad_hidden * gate_act).astype(jnp.bfloat16)
    contribution = contract_cols(
        grad_gate, lax.all_gather(w_gate, "fsdp", axis=0, tiled=True)
    ) + contract_cols(grad_up, lax.all_gather(w_up, "fsdp", axis=0, tiled=True))
    grad_gain_two = jnp.sum(contribution * unit_two, axis=0)
    grad_resid = grad_out + norm_back(contribution, unit_two, factor_two, gain_two)
    grad_branch = grad_resid.astype(jnp.bfloat16)
    attn_again = (
        lax.all_gather(w_qkv, "fsdp", axis=0, tiled=True),
        lax.all_gather(w_hgate, "fsdp", axis=0, tiled=True),
        lax.all_gather(w_out, "fsdp", axis=0, tiled=True),
    )
    grad_gated = matmul(grad_branch, attn_again[2]).reshape(count_of_rows, QUERY_HEADS, HEAD_SIZE)
    grad_heads = (
        (grad_gated * head_gate[:, :, None])
        .astype(jnp.bfloat16)
        .reshape(count_of_rows, KEY_VALUE_HEADS, group_list, HEAD_SIZE)
    )
    grad_logit = (jnp.sum(grad_gated * head_out, axis=-1) * head_gate * (1.0 - head_gate)).astype(
        jnp.bfloat16
    )
    probs_again = jnp.exp(attention_scores(queries, keys_rot, allowed) - log_total)
    grad_probs = jnp.einsum(
        "qkgd,pkd->kgqp", grad_heads, value_rows, preferred_element_type=jnp.float32
    )
    value_gradient = jnp.einsum(
        "kgqp,qkgd->pkd",
        probs_again.astype(jnp.bfloat16),
        grad_heads,
        preferred_element_type=jnp.float32,
    )
    grad_scores = (
        probs_again * (grad_probs - jnp.sum(probs_again * grad_probs, axis=-1, keepdims=True))
    ).astype(jnp.bfloat16)
    grad_queries = (
        jnp.einsum("kgqp,pkd->qkgd", grad_scores, keys_rot, preferred_element_type=jnp.float32)
        * HEAD_SIZE ** (-0.5)
    ).astype(jnp.bfloat16)
    grad_keys = (
        jnp.einsum("kgqp,qkgd->pkd", grad_scores, queries, preferred_element_type=jnp.float32)
        * HEAD_SIZE ** (-0.5)
    ).astype(jnp.bfloat16)
    grad_query_rot = unrotate(
        grad_queries.astype(jnp.float32).reshape(count_of_rows, QUERY_HEADS, HEAD_SIZE),
        cosine,
        sine_table,
    )
    grad_key_rot = unrotate(grad_keys.astype(jnp.float32), cosine, sine_table)
    grad_query_gain = jnp.sum(grad_query_rot * query_unit, axis=(0, 1))
    grad_key_gain = jnp.sum(grad_key_rot * key_unit, axis=(0, 1))
    grad_query_raw = norm_back(grad_query_rot, query_unit, query_factor, query_gain)
    gradient_key_unrotated = norm_back(grad_key_rot, key_unit, key_factor, key_gain)
    grad_projected = jnp.concatenate(
        [
            grad_query_raw.reshape(count_of_rows, QUERY_HEADS * HEAD_SIZE),
            gradient_key_unrotated.reshape(count_of_rows, KEY_VALUE_HEADS * HEAD_SIZE),
            value_gradient.reshape(count_of_rows, KEY_VALUE_HEADS * HEAD_SIZE),
        ],
        axis=1,
    ).astype(jnp.bfloat16)
    grad_normed_one = contract_cols(grad_projected, attn_again[0]) + contract_cols(
        grad_logit, attn_again[1]
    )
    grad_gain_one = jnp.sum(grad_normed_one * unit_one, axis=0)
    grad_stream = grad_resid + norm_back(grad_normed_one, unit_one, factor_one, gain_one)
    returned = pick_rows(
        target,
        (blank, blank),
        (
            lax.all_gather(final_rows, "fsdp", axis=0, tiled=True),
            lax.all_gather(grad_stream.astype(jnp.bfloat16), "fsdp", axis=0, tiled=True),
        ),
    )
    cot_cols = dealt_cot
    mlp_grad = lax.psum_scatter(
        jnp.concatenate(
            [
                contract_rows(normed_two, grad_gate),
                contract_rows(normed_two, grad_up),
                contract_rows(cot_cols, hidden),
            ],
            axis=1,
        ),
        ("fsdp", "rep"),
        scatter_dimension=0,
        tiled=True,
    )
    attn_grad = lax.psum_scatter(
        jnp.concatenate(
            [contract_rows(normed_one, grad_projected), contract_rows(grad_branch, gated)], axis=1
        ),
        ("fsdp", "rep"),
        scatter_dimension=0,
        tiled=True,
    )
    mlp_grad, attn_grad = (
        lax.all_gather(mlp_grad.astype(jnp.bfloat16), "rep", axis=0, tiled=True).astype(
            mlp_grad.dtype
        ),
        lax.all_gather(attn_grad.astype(jnp.bfloat16), "rep", axis=0, tiled=True).astype(
            attn_grad.dtype
        ),
    )
    grad_hgate = contract_rows(normed_one, grad_logit)
    small = lax.psum(
        (grad_gain_one, grad_gain_two, grad_query_gain, grad_key_gain, grad_hgate), ("fsdp", "rep")
    )

    def own_rows(full_rows):
        piece_rows = full_rows.shape[0] // devices_fsdp
        return lax.dynamic_slice_in_dim(full_rows, shard * piece_rows, piece_rows, 0)

    qkv_cols = w_qkv.shape[1]
    return (
        returned[0][None],
        returned[1][None],
        own_rows(small[0]),
        own_rows(small[1]),
        own_rows(small[2]),
        own_rows(small[3]),
        attn_grad[:, :qkv_cols],
        own_rows(small[4]),
        attn_grad[:, qkv_cols:],
        mlp_grad[:, :FF],
        mlp_grad[:, FF : 2 * FF],
        mlp_grad[:, 2 * FF :],
    )


def solution(mesh):
    return jax.shard_map(
        on_device,
        mesh=mesh,
        in_specs=(
            P("rep", "fsdp", None),
            P("rep", "fsdp", None),
            P("rep", None),
            P("rep", None),
            P("fsdp"),
            P("fsdp"),
            P("fsdp"),
            P("fsdp"),
            P("fsdp", None),
            P("fsdp", None),
            P("fsdp", None),
            P("fsdp", None),
            P("fsdp", None),
            P("fsdp", None),
        ),
        out_specs=(
            P("rep", "fsdp", None),
            P("rep", "fsdp", None),
            P("fsdp"),
            P("fsdp"),
            P("fsdp"),
            P("fsdp"),
            P("fsdp", None),
            P("fsdp", None),
            P("fsdp", None),
            P("fsdp", None),
            P("fsdp", None),
            P("fsdp", None),
        ),
        check_vma=False,
    )
```

profile of v0, /device:TPU:0, one launch (start us, length us, event | category | flops | bytes accessed | tf_op | source)
XLA Modules:
  0.0 4046.7 jit_solution(8224755430427772333)
XLA Ops:
  14.1 13.8 all-reduce.3
  28.4 12.7 all-gather.1
  41.7 12.6 all-gather
  57.4 13.2 all_gather.59
  76.0 28.8 all-gather.14.cloned.1.call-done
  109.4 282.5 %all-gather.16.cloned.1.call-done = bf16[2048,4096]{1,0:T(8,128)(2,1)} async-done(((bf16[512,4096]{1,0:T(8,128)(2,1)}), bf16[2048,4096]{1,0:T(8,128)(2,1)}) %all-gather.16.cloned.1.call-update) | async-done | bytes 16777232 | tf_op jit(solution)/shard_map/all_gather | solution.py:152
  408.5 132.7 %all-gather.18.cloned.1.call-done = bf16[2048,2048]{1,0:T(8,128)(2,1)} async-done(((bf16[512,2048]{1,0:T(8,128)(2,1)}), bf16[2048,2048]{1,0:T(8,128)(2,1)}) %all-gather.18.cloned.1.call-update) | async-done | bytes 8388624 | tf_op jit(solution)/shard_map/all_gather | solution.py:154
  549.4 416.6 %all-gather.22.cloned.1.call-done = bf16[2048,6144]{1,0:T(8,128)(2,1)} async-done(((bf16[512,6144]{1,0:T(8,128)(2,1)}), bf16[2048,6144]{1,0:T(8,128)(2,1)}) %all-gather.22.cloned.1.call-update) | async-done | bytes 25165840 | tf_op jit(solution)/shard_map/all_gather | solution.py:210
  966.0 15.6 fusion.74
  981.6 409.2 %all-gather.20.cloned.1.call-done = bf16[2048,6144]{1,0:T(8,128)(2,1)} async-done(((bf16[512,6144]{1,0:T(8,128)(2,1)}), bf16[2048,6144]{1,0:T(8,128)(2,1)}) %all-gather.20.cloned.1.call-update) | async-done | bytes 25165840 | tf_op jit(solution)/shard_map/all_gather | solution.py:209
  1390.8 15.0 fusion.73
  1405.7 410.0 %all-gather.24.cloned.1.call-done = bf16[2048,6144]{1,0:T(8,128)(2,1)} async-done(((bf16[512,6144]{1,0:T(8,128)(2,1)}), bf16[2048,6144]{1,0:T(8,128)(2,1)}) %all-gather.24.cloned.1.call-update) | async-done | bytes 25165840 | tf_op jit(solution)/shard_map/all_gather | solution.py:211
  1815.7 14.7 multiply_convert_fusion
  1830.4 14.3 fusion.75
  1844.7 15.5 multiply_reduce_fusion.1
  1910.1 13.3 fusion.43
  1923.4 33.6 pad_maximum_fusion.1
  1958.1 31.9 fusion.77
  1990.0 30.2 fusion.76
  2020.2 22.4 fusion.67
  2042.6 100.4 %pad_maximum_fusion = f32[2048,18432]{1,0:T(8,128)} fusion(f32[2048,6144]{1,0:T(8,128)} %fusion.67, f32[2048,6144]{1,0:T(8,128)} %fusion.77, f32[2048,6144]{1,0:T(8,128)} %fusion.76), kind=kLoop, calls=%fused_computation.4 | loop fusion | flops 75497472 | bytes 301989888 | tf_op jit(solution)/shard_map/concatenate | solution.py:300
  2145.2 14.5 fusion.1
  2159.8 12.0 fusion.44
  2173.6 211.0 %reduce-scatter.3.cloned.1.call-done = f32[64,6144]{1,0:T(8,128)} async-done(((f32[2048,6144]{1,0:T(8,128)}), f32[64,6144]{1,0:T(8,128)}) %reduce-scatter.3.cloned.1.call-update) | async-done | bytes 1572880 | tf_op jit(solution)/shard_map/reduce_scatter | solution.py:312
  2387.1 1264.7 %reduce-scatter.5.cloned.1.call-done = f32[64,18432]{1,0:T(8,128)} async-done(((f32[2048,18432]{1,0:T(8,128)}), f32[64,18432]{1,0:T(8,128)}) %reduce-scatter.5.cloned.1.call-update) | async-done | bytes 4718608 | tf_op jit(solution)/shard_map/reduce_scatter | solution.py:299
  3655.9 40.0 all-reduce.2
  3698.4 83.2 %all-reduce.6.cloned.1.call-done = f32[2048,16]{0,1:T(8,128)} async-done(((f32[2048,16]{0,1:T(8,128)}), f32[2048,16]{0,1:T(8,128)}) %all-reduce.6.cloned.1.call-update) | async-done | bytes 131088 | tf_op jit(solution)/shard_map/psum | solution.py:329
  3782.9 45.5 %all-gather.26.cloned.1.call-done = bf16[512,2048]{1,0:T(8,128)(2,1)} async-done(((bf16[128,2048]{1,0:T(8,128)(2,1)}), bf16[512,2048]{1,0:T(8,128)(2,1)}) %all-gather.26.cloned.1.call-update) | async-done | bytes 2097168 | tf_op jit(solution)/shard_map/all_gather | solution.py:294
  3831.7 43.2 %all-gather.30.cloned.1.call-done = bf16[512,2048]{1,0:T(8,128)(2,1)} async-done(((bf16[128,2048]{1,0:T(8,128)(2,1)}), bf16[512,2048]{1,0:T(8,128)(2,1)}) %all-gather.30.cloned.1.call-update) | async-done | bytes 2097168 | tf_op jit(solution)/shard_map/all_gather | solution.py:295
  3879.4 42.2 %all-gather.32.cloned.1.call-done = bf16[512,6144]{1,0:T(8,128)(2,1)} async-done(((bf16[64,6144]{1,0:T(8,128)(2,1)}), bf16[512,6144]{1,0:T(8,128)(2,1)}) %all-gather.32.cloned.1.call-update) | async-done | bytes 6291472 | tf_op jit(solution)/shard_map/all_gather | solution.py:324
  3930.4 92.2 %all-gather.34.cloned.1.call-done = bf16[512,18432]{1,0:T(8,128)(2,1)} async-done(((bf16[64,18432]{1,0:T(8,128)(2,1)}), bf16[512,18432]{1,0:T(8,128)(2,1)}) %all-gather.34.cloned.1.call-update) | async-done | bytes 18874384 | tf_op jit(solution)/shard_map/all_gather | solution.py:321
  4022.5 17.5 fusion.69
  (276 shorter events, 126.3 us)
Async XLA Ops:
  7.2 64.7 %all-gather.28.cloned.1.call-start = ((), (), s32[]{:S(2)}) async-start(), calls=%async_computation.9 | async-start | bytes 2621440 | tf_op jit(solution)/shard_map/all_gather | solution.py:144
  7.9 96.8 %all-gather.14.cloned.1.call-start = ((), (), s32[]{:S(2)}) async-start(), calls=%async_computation.2 | async-start | bytes 2621440 | tf_op jit(solution)/shard_map/all_gather | solution.py:143
  8.7 383.2 %all-gather.16.cloned.1.call-start = ((), (), s32[]{:S(2)}) async-start(), calls=%async_computation.3 | async-start | bytes 20971520 | tf_op jit(solution)/shard_map/all_gather | solution.py:152
  9.4 531.8 %all-gather.18.cloned.1.call-start = ((), (), s32[]{:S(2)}) async-start(), calls=%async_computation.4 | async-start | bytes 10485760 | tf_op jit(solution)/shard_map/all_gather | solution.py:154
  10.0 956.0 %all-gather.22.cloned.1.call-start = ((), (), s32[]{:S(2)}) async-start(), calls=%async_computation.6 | async-start | bytes 31457280 | tf_op jit(solution)/shard_map/all_gather | solution.py:210
  10.6 1380.2 %all-gather.20.cloned.1.call-start = ((), (), s32[]{:S(2)}) async-start(), calls=%async_computation.5 | async-start | bytes 31457280 | tf_op jit(solution)/shard_map/all_gather | solution.py:209
  11.2 46.2 %copy-start.50 = (bf16[512,16]{0,1:T(8,128)(2,1)S(1)}, bf16[512,16]{0,1:T(8,128)(2,1)}, u32[]{:S(2)}) copy-start(bf16[512,16]{0,1:T(8,128)(2,1)} %param.25) | copy-start | bytes 49156
  11.2 1804.5 %all-gather.24.cloned.1.call-start = ((), (), s32[]{:S(2)}) async-start(), calls=%async_computation.7 | async-start | bytes 31457280 | tf_op jit(solution)/shard_map/all_gather | solution.py:211
  12.0 2372.7 %reduce-scatter.3.cloned.1.call-start = ((), (), s32[]{:S(2)}) async-start(), calls=%async_computation.11 | async-start | bytes 51904512 | tf_op jit(solution)/shard_map/reduce_scatter | solution.py:312
  27.9 376.1 %copy-start.53 = (f32[128]{0:T(128)}, f32[128]{0:T(128)S(1)}, u32[]{:S(2)}) copy-start(f32[128]{0:T(128)S(1)} %convert_element_type.131) | copy-start | bytes 1540
  27.9 80.1 %copy-start.51 = (f32[128]{0:T(128)}, f32[128]{0:T(128)S(1)}, u32[]{:S(2)}) copy-start(f32[128]{0:T(128)S(1)} %convert_element_type.134) | copy-start | bytes 1540
  54.3 1855.0 %copy-start.25 = (f32[4,1,512]{2,1,0:T(1,128)}, f32[4,1,512]{2,1,0:T(1,128)S(1)}, u32[]{:S(2)}) copy-start(f32[4,1,512]{2,1,0:T(1,128)S(1)} %convert_element_type.163) | copy-start | bytes 24580
  70.5 37.9 copy-start.27
  70.5 37.5 copy-start.46
  70.6 37.5 copy-start.48
  108.4 291.7 %copy-start.3 = (bf16[128,2048]{1,0:T(8,128)(2,1)}, bf16[128,2048]{1,0:T(8,128)(2,1)S(1)}, u32[]{:S(2)}) copy-start(bf16[128,2048]{1,0:T(8,128)(2,1)S(1)} %get-tuple-element.43) | copy-start | bytes 1572868
  108.4 291.7 %copy-start.43 = (f32[128]{0:T(128)}, f32[128]{0:T(128)S(1)}, u32[]{:S(2)}) copy-start(f32[128]{0:T(128)S(1)} %add_rsqrt_fusion.3) | copy-start | bytes 1540
  547.7 1313.1 %copy-start = (f32[128,2048]{1,0:T(8,128)}, f32[128,2048]{1,0:T(8,128)S(1)}, u32[]{:S(2)}) copy-start(f32[128,2048]{1,0:T(8,128)S(1)} %get-tuple-element.68) | copy-start | bytes 3145732
  1957.1 32.9 copy-start.12
  1957.1 1694.7 %reduce-scatter.5.cloned.1.call-start = ((), (), s32[]{:S(2)}) async-start(), calls=%async_computation.14 | async-start | bytes 155713536 | tf_op jit(solution)/shard_map/reduce_scatter | solution.py:299
  1990.0 30.2 copy-start.47
  1990.0 30.2 copy-start.49
  2143.1 1638.4 %all-reduce.6.cloned.1.call-start = ((), (), s32[]{:S(2)}) async-start(), calls=%async_computation.13 | async-start | bytes 262144 | tf_op jit(solution)/shard_map/psum | solution.py:329
  2145.1 1683.3 %all-gather.26.cloned.1.call-start = ((), (), s32[]{:S(2)}) async-start(), calls=%async_computation.8 | async-start | bytes 2621440 | tf_op jit(solution)/shard_map/all_gather | solution.py:294
  2159.7 1715.2 %all-gather.30.cloned.1.call-start = ((), (), s32[]{:S(2)}) async-start(), calls=%async_computation.10 | async-start | bytes 2621440 | tf_op jit(solution)/shard_map/all_gather | solution.py:295
  2173.6 1748.0 %all-gather.32.cloned.1.call-start = ((), (), s32[]{:S(2)}) async-start(), calls=%async_computation.12 | async-start | bytes 7077888 | tf_op jit(solution)/shard_map/all_gather | solution.py:324
  2387.0 1268.8 %copy-start.56 = (s32[128]{0:T(128)S(1)}, s32[128]{0:T(128)}, u32[]{:S(2)}) copy-start(s32[128]{0:T(128)} %get-tuple-element.25) | copy-start | bytes 1540
  2387.0 1268.8 %copy-start.57 = (s32[128]{0:T(128)S(1)}, s32[128]{0:T(128)}, u32[]{:S(2)}) copy-start(s32[128]{0:T(128)} %get-tuple-element.21) | copy-start | bytes 1540
  2387.0 1268.8 %copy-start.41 = (f32[2048]{0:T(1024)S(1)}, f32[2048]{0:T(1024)}, u32[]{:S(2)}) copy-start(f32[2048]{0:T(1024)} %get-tuple-element.15) | copy-start | bytes 24580
  2387.1 1268.8 %copy-start.55 = (f32[128]{0:T(128)S(1)}, f32[128]{0:T(128)}, u32[]{:S(2)}) copy-start(f32[128]{0:T(128)} %get-tuple-element.13) | copy-start | bytes 1540
  2387.1 1268.8 %copy-start.58 = (f32[128]{0:T(128)S(1)}, f32[128]{0:T(128)}, u32[]{:S(2)}) copy-start(f32[128]{0:T(128)} %get-tuple-element.19) | copy-start | bytes 1540
  2387.1 1635.5 %all-gather.34.cloned.1.call-start = ((), (), s32[]{:S(2)}) async-start(), calls=%async_computation.15 | async-start | bytes 21233664 | tf_op jit(solution)/shard_map/all_gather | solution.py:321
  (48 other events, 274.4 us)
Sparse Core Ops, SparseCore 0:
  9.6 49.0 all-gather.27
  60.2 44.4 all-gather.13
  106.3 285.5 all-gather.15
  393.3 147.7 all-gather.17
  542.6 423.3 all-gather.21
  967.4 423.3 all-gather.19
  1392.4 423.3 all-gather.23
  1957.2 427.3 reduce-scatter.2
  2391.1 1260.6 reduce-scatter.4
  3657.8 123.7 all-reduce.5
  3783.7 44.6 all-gather.25
  3830.4 44.4 all-gather.29
  3877.4 44.1 all-gather.31
  3923.9 98.5 all-gather.33
where the time goes:
time: 4060 us; the launch traced here: 4050 us
  waiting for transfers between devices  3470 us (85%)
  matrix products  237 us (6%)
  other arithmetic  170 us (4%)
  blocking collectives  92.2 us (2%)
  local copies, waits for them, and re-layouts  64.8 us (2%)
    reduce_scatter x1, waiting for transfers between devices, on_device(): lax.psum_scatter(jnp.concatenate([contract_rows(normed_two, grad_gate), c...  1260 us
    all_gather x1, waiting for transfers between devices, on_device(): lax.all_gather(w_up, 'fsdp', axis=0, tiled=True)  417 us
    all_gather x1, waiting for transfers between devices, on_device(): lax.all_gather(w_down, 'fsdp', axis=0, tiled=True)  410 us
    all_gather x1, waiting for transfers between devices, on_device(): lax.all_gather(w_gate, 'fsdp', axis=0, tiled=True)  409 us
    all_gather x1, waiting for transfers between devices, on_device(): lax.all_gather(w_qkv, 'fsdp', axis=0, tiled=True)  283 us
    reduce_scatter x1, waiting for transfers between devices, on_device(): lax.psum_scatter(jnp.concatenate([contract_rows(normed_one, grad_projecte...  211 us
    all_gather x1, waiting for transfers between devices, on_device(): lax.all_gather(w_out, 'fsdp', axis=0, tiled=True)  133 us
    dot_general x6, matrix products, contract_rows(): lax.dot_general(left, right, (((0,), (0,)), ((), ())), preferred_element_...  108 us
  transfers between devices with their start and end apart: 14, of which 13 were waited for; matrix products, arithmetic and copies ran while one was open for 8% of the time, Pallas kernels for 0%

commit v1 on v0

v1 whole, which is shorter than its diff:
```python
import jax
import jax.numpy as jnp
from jax import lax
from jax.sharding import PartitionSpec as P

QUERY_HEADS = 16
KEY_VALUE_HEADS = 8
HEAD_SIZE = 128
FF = 6144


eps_norm = 1e-06
rope_base = 1000000.0


def matmul(left, right):
    return jnp.dot(left, right, preferred_element_type=jnp.float32)


def contract_rows(left, right):
    return lax.dot_general(
        left, right, (((0,), (0,)), ((), ())), preferred_element_type=jnp.float32
    )


def contract_cols(left, right):
    return lax.dot_general(
        left, right, (((1,), (1,)), ((), ())), preferred_element_type=jnp.float32
    )


def normalize(value_rows):
    factor = lax.rsqrt(jnp.mean(value_rows * value_rows, axis=-1, keepdims=True) + eps_norm)
    return (value_rows * factor, factor)


def norm_back(grad_normed, normed_unit, factor, gain):
    scaled = grad_normed * gain
    return factor * (scaled - normed_unit * jnp.mean(scaled * normed_unit, axis=-1, keepdims=True))


def rope_tables(positions):
    half_dim = HEAD_SIZE // 2
    frequency = jnp.power(rope_base, -2.0 * jnp.arange(half_dim, dtype=jnp.float32) / HEAD_SIZE)
    angles = positions.astype(jnp.float32)[:, None] * frequency[None, :]
    angles = jnp.concatenate([angles, angles], axis=1)
    return (jnp.cos(angles)[:, None, :], jnp.sin(angles)[:, None, :])


def rotate(value_rows, cosine, sine_table):
    half_dim = value_rows.shape[-1] // 2
    turned = jnp.concatenate([-value_rows[..., half_dim:], value_rows[..., :half_dim]], axis=-1)
    return value_rows * cosine + turned * sine_table


def unrotate(grads, cosine, sine_table):
    half_dim = grads.shape[-1] // 2
    shifted = grads * sine_table
    turned = jnp.concatenate([shifted[..., half_dim:], -shifted[..., :half_dim]], axis=-1)
    return grads * cosine + turned


LANES = 8
HALO = 64
BITS = (2, 4, 1)


def exchange(value, bit):
    count = lax.axis_size("rep")
    return lax.ppermute(value, "rep", [(i, i ^ bit) for i in range(count)])


def plane_gather(rows):
    for bit in BITS:
        rows = jnp.concatenate([rows, exchange(rows, bit)], axis=0)
    return rows


def plane_scatter(partial):
    for bit in reversed(BITS):
        half = partial.shape[0] // 2
        arrived = exchange(partial[half:].astype(jnp.bfloat16), bit)
        partial = partial[:half] + arrived.astype(jnp.float32)
    return partial


def plane_groups():
    count = lax.axis_size("rep")
    if count == LANES:
        return None
    return [list(range(first, first + LANES)) for first in range(0, count, LANES)]


def sum_owned(partial):
    total = lax.psum_scatter(
        partial.astype(jnp.bfloat16), "fsdp", scatter_dimension=0, tiled=True
    )
    bit = LANES
    while bit < lax.axis_size("rep"):
        total = (total.astype(jnp.float32) + exchange(total, bit).astype(jnp.float32)).astype(
            jnp.bfloat16
        )
        bit *= 2
    return total


def all_columns(owned):
    return lax.all_gather(owned, "rep", axis=0, axis_index_groups=plane_groups())


def side_by_side(blocks):
    lanes, rows, columns = blocks.shape
    return blocks.transpose(1, 0, 2).reshape(rows, lanes * columns).astype(jnp.float32)


def take_cols(weight, first, count):
    return lax.dynamic_slice_in_dim(weight, first, count, 1)


def on_device(
    tokens,
    cotangent,
    lengths,
    deal_order,
    attn_gain,
    mlp_gain,
    q_scale,
    k_scale,
    w_qkv,
    w_hgate,
    w_out,
    w_gate,
    w_up,
    w_down,
):
    f32, bf16 = jnp.float32, jnp.bfloat16
    rows = tokens.shape[1]
    width = tokens.shape[2]
    shards = lax.axis_size("fsdp")
    shard = lax.axis_index("fsdp")
    lane = lax.rem(lax.axis_index("rep"), LANES)
    group_list = QUERY_HEADS // KEY_VALUE_HEADS
    q_cols = group_list * HEAD_SIZE
    ff_cols = w_gate.shape[1] // LANES
    out_rows = w_out.shape[0]

    def padded(vector):
        return jnp.pad(vector, (0, out_rows - vector.shape[0]))[:, None]

    weights_one = jnp.concatenate(
        [
            take_cols(w_qkv, lane * q_cols, q_cols),
            take_cols(w_qkv, QUERY_HEADS * HEAD_SIZE + lane * HEAD_SIZE, HEAD_SIZE),
            take_cols(
                w_qkv, (QUERY_HEADS + KEY_VALUE_HEADS) * HEAD_SIZE + lane * HEAD_SIZE, HEAD_SIZE
            ),
            jnp.pad(
                jnp.concatenate(
                    [
                        take_cols(w_hgate, lane * group_list, group_list),
                        attn_gain[:, None],
                        mlp_gain[:, None],
                        padded(q_scale),
                        padded(k_scale),
                    ],
                    axis=1,
                ),
                ((0, 0), (0, 128 - group_list - 4)),
            ),
            take_cols(w_out, lane * q_cols, q_cols),
        ],
        axis=1,
    )
    weights_one = lax.all_gather(weights_one, "fsdp", axis=0, tiled=True)
    weights_two = lax.all_gather(
        jnp.concatenate(
            [take_cols(w_gate, lane * ff_cols, ff_cols), take_cols(w_up, lane * ff_cols, ff_cols)],
            axis=1,
        ),
        "fsdp",
        axis=0,
        tiled=True,
    )
    weights_three = lax.all_gather(
        take_cols(w_down, lane * ff_cols, ff_cols), "fsdp", axis=0, tiled=True
    )
    qkv_cols = q_cols + 2 * HEAD_SIZE
    w_in = weights_one[:, : qkv_cols + 128]
    w_attn = weights_one[:, qkv_cols + 128 :]
    extra = weights_one[:, qkv_cols : qkv_cols + group_list + 4].astype(f32)
    gain_one = extra[:, group_list]
    gain_two = extra[:, group_list + 1]
    scales = extra.reshape(shards, width // shards, group_list + 4)[:, : HEAD_SIZE // shards]
    query_gain = scales[:, :, group_list + 2].reshape(HEAD_SIZE)
    key_gain = scales[:, :, group_list + 3].reshape(HEAD_SIZE)

    seq_lengths = lengths[0]
    ends = jnp.cumsum(seq_lengths)
    starts = ends - seq_lengths
    own_index = shard * rows + jnp.arange(rows, dtype=jnp.int32)
    begun = own_index[:, None] >= starts[None, :]
    own_position = own_index - jnp.max(jnp.where(begun, starts[None, :], 0), axis=1)

    own_x = tokens[0]
    own_dy = cotangent[0]
    gathered = plane_gather(
        jnp.concatenate(
            [own_x, jnp.broadcast_to(own_position.astype(bf16)[:, None], (rows, 128))], axis=1
        )
    )
    stream_all = gathered[:, :width].astype(f32)
    position = gathered[:, width].astype(jnp.int32)
    cot_all = plane_gather(own_dy)
    total_rows = LANES * rows

    normed_one = (normalize(stream_all)[0] * gain_one).astype(bf16)
    projected = matmul(normed_one, w_in)
    head_logit = projected[:, qkv_cols : qkv_cols + group_list]
    query_raw = projected[:, :q_cols].reshape(total_rows, group_list, HEAD_SIZE)
    key_raw = projected[:, q_cols : q_cols + HEAD_SIZE].reshape(total_rows, 1, HEAD_SIZE)
    values = projected[:, q_cols + HEAD_SIZE : qkv_cols].astype(bf16)
    query_unit, query_factor = normalize(query_raw)
    key_unit, key_factor = normalize(key_raw)
    cosine, sine_table = rope_tables(position)
    queries = (
        rotate(query_unit * query_gain, cosine, sine_table)
        .astype(bf16)
        .reshape(LANES, rows, group_list, HEAD_SIZE)
        .transpose(0, 2, 1, 3)
        .reshape(LANES, group_list * rows, HEAD_SIZE)
    )
    keys = rotate(key_unit * key_gain, cosine, sine_table).astype(bf16)
    key_value = jnp.concatenate([keys.reshape(total_rows, HEAD_SIZE), values], axis=1).reshape(
        LANES, rows, 2 * HEAD_SIZE
    )
    before = lax.ppermute(
        key_value[:, rows - HALO :], "fsdp", [(i, i + 1) for i in range(shards - 1)]
    )
    key_value = jnp.concatenate([before, key_value], axis=1)
    keys_wide = key_value[:, :, :HEAD_SIZE]
    values_wide = key_value[:, :, HEAD_SIZE:]
    local = jnp.arange(rows, dtype=jnp.int32)
    offset = jnp.arange(HALO + rows, dtype=jnp.int32) - HALO
    allowed = (offset[None, None, :] <= local[None, :, None]) & (
        offset[None, None, :] >= local[None, :, None] - position.reshape(LANES, rows)[:, :, None]
    )
    scores = jnp.einsum(
        "sqd,spd->sqp", queries, keys_wide, preferred_element_type=f32
    ) * HEAD_SIZE ** (-0.5)
    scores = jnp.where(jnp.concatenate([allowed] * group_list, axis=1), scores, -1e30)
    weights_exp = jnp.exp(scores - jnp.max(scores, axis=-1, keepdims=True))
    probs = weights_exp / jnp.sum(weights_exp, axis=-1, keepdims=True)
    probs_low = probs.astype(bf16)

    def by_row(value):
        return (
            value.reshape(LANES, group_list, rows, HEAD_SIZE)
            .transpose(0, 2, 1, 3)
            .reshape(total_rows, group_list, HEAD_SIZE)
        )

    def by_head(value):
        return (
            value.reshape(LANES, rows, group_list, HEAD_SIZE)
            .transpose(0, 2, 1, 3)
            .reshape(LANES, group_list * rows, HEAD_SIZE)
        )

    head_out = by_row(
        jnp.einsum("sqp,spd->sqd", probs_low, values_wide, preferred_element_type=f32)
    )
    head_gate = jax.nn.sigmoid(head_logit)
    gated = (head_out * head_gate[:, :, None]).astype(bf16).reshape(total_rows, q_cols)
    residual = own_x.astype(f32) + plane_scatter(contract_cols(gated, w_attn))
    unit_two, factor_two = normalize(residual)
    normed_two = plane_gather((unit_two * gain_two).astype(bf16))
    pre = matmul(normed_two, weights_two)
    gate_pre = pre[:, :ff_cols]
    up_pre = pre[:, ff_cols:]
    gate_sig = jax.nn.sigmoid(gate_pre)
    gate_act = gate_pre * gate_sig
    hidden = (gate_act * up_pre).astype(bf16)
    down_sum = sum_owned(contract_rows(cot_all, hidden))
    final_rows = residual + plane_scatter(contract_cols(hidden, weights_three))

    grad_hidden = matmul(cot_all, weights_three)
    grad_pre = jnp.concatenate(
        [
            (grad_hidden * up_pre * gate_sig * (1.0 + gate_pre * (1.0 - gate_sig))).astype(bf16),
            (grad_hidden * gate_act).astype(bf16),
        ],
        axis=1,
    )
    pre_sum = sum_owned(contract_rows(normed_two, grad_pre))
    contribution = plane_scatter(contract_cols(grad_pre, weights_two))
    grad_gain_two = jnp.sum(contribution * unit_two, axis=0)
    grad_resid = own_dy.astype(f32) + norm_back(contribution, unit_two, factor_two, gain_two)
    grad_branch = plane_gather(grad_resid.astype(bf16))
    grad_gated = matmul(grad_branch, w_attn).reshape(total_rows, group_list, HEAD_SIZE)
    grad_heads = by_head((grad_gated * head_gate[:, :, None]).astype(bf16))
    grad_logit = (jnp.sum(grad_gated * head_out, axis=-1) * head_gate * (1.0 - head_gate)).astype(
        bf16
    )
    grad_probs = jnp.einsum("sqd,spd->sqp", grad_heads, values_wide, preferred_element_type=f32)
    grad_values = jnp.einsum("sqp,sqd->spd", probs_low, grad_heads, preferred_element_type=f32)
    grad_scores = (
        probs * (grad_probs - jnp.sum(probs * grad_probs, axis=-1, keepdims=True))
    ).astype(bf16)
    grad_queries = (
        jnp.einsum("sqp,spd->sqd", grad_scores, keys_wide, preferred_element_type=f32)
        * HEAD_SIZE ** (-0.5)
    ).astype(bf16)
    grad_keys = jnp.einsum("sqp,sqd->spd", grad_scores, queries, preferred_element_type=f32)
    grad_key_value = jnp.concatenate([grad_keys, grad_values], axis=2)
    after = lax.ppermute(
        grad_key_value[:, :HALO].astype(bf16), "fsdp", [(i + 1, i) for i in range(shards - 1)]
    )
    grad_key_value = grad_key_value[:, HALO:] + jnp.pad(
        after.astype(f32), ((0, 0), (rows - HALO, 0), (0, 0))
    )
    grad_keys = (grad_key_value[:, :, :HEAD_SIZE] * HEAD_SIZE ** (-0.5)).astype(bf16)
    grad_values = grad_key_value[:, :, HEAD_SIZE:].reshape(total_rows, HEAD_SIZE)
    grad_query_rot = unrotate(by_row(grad_queries).astype(f32), cosine, sine_table)
    grad_key_rot = unrotate(
        grad_keys.astype(f32).reshape(total_rows, 1, HEAD_SIZE), cosine, sine_table
    )
    grad_query_gain = jnp.sum(grad_query_rot * query_unit, axis=(0, 1))
    grad_key_gain = jnp.sum(grad_key_rot * key_unit, axis=(0, 1))
    grad_query_raw = norm_back(grad_query_rot, query_unit, query_factor, query_gain)
    grad_key_raw = norm_back(grad_key_rot, key_unit, key_factor, key_gain)
    grad_projected = jnp.concatenate(
        [
            grad_query_raw.reshape(total_rows, q_cols),
            grad_key_raw.reshape(total_rows, HEAD_SIZE),
            grad_values,
            jnp.pad(grad_logit.astype(f32), ((0, 0), (0, 128 - group_list))),
        ],
        axis=1,
    ).astype(bf16)

    grad_normed_one = plane_scatter(contract_cols(grad_projected, w_in))
    grad_in = contract_rows(normed_one, grad_projected)
    attn_sum = sum_owned(
        jnp.concatenate([grad_in[:, :qkv_cols], contract_rows(grad_branch, gated)], axis=1)
    )
    unit_one, factor_one = normalize(own_x.astype(f32))
    grad_gain_one = jnp.sum(grad_normed_one * unit_one, axis=0)
    grad_stream = grad_resid + norm_back(grad_normed_one, unit_one, factor_one, gain_one)

    lane_mask = (jnp.arange(LANES) == lane).astype(f32)
    grad_hgate = grad_in[:, qkv_cols : qkv_cols + group_list].T
    small = jnp.concatenate(
        [
            (lane_mask[:, None, None] * grad_hgate[None]).reshape(QUERY_HEADS, width),
            grad_gain_one[None],
            grad_gain_two[None],
            jnp.pad(grad_query_gain, (0, width - HEAD_SIZE))[None],
            jnp.pad(grad_key_gain, (0, width - HEAD_SIZE))[None],
            jnp.zeros((4, width), f32),
        ],
        axis=0,
    )
    small = lax.psum(small, ("fsdp", "rep"))

    def own_part(vector):
        piece = vector.shape[-1] // shards
        return lax.dynamic_slice_in_dim(vector, shard * piece, piece, vector.ndim - 1)

    down_all = all_columns(down_sum)
    pre_all = all_columns(pre_sum)
    attn_all = all_columns(attn_sum)
    return (
        final_rows.astype(bf16)[None],
        grad_stream.astype(bf16)[None],
        own_part(small[QUERY_HEADS]),
        own_part(small[QUERY_HEADS + 1]),
        own_part(small[QUERY_HEADS + 2, :HEAD_SIZE]),
        own_part(small[QUERY_HEADS + 3, :HEAD_SIZE]),
        jnp.concatenate(
            [
                side_by_side(attn_all[:, :, :q_cols]),
                side_by_side(attn_all[:, :, q_cols : q_cols + HEAD_SIZE]),
                side_by_side(attn_all[:, :, q_cols + HEAD_SIZE : qkv_cols]),
            ],
            axis=1,
        ),
        own_part(small[:QUERY_HEADS]).T,
        side_by_side(attn_all[:, :, qkv_cols:]),
        side_by_side(pre_all[:, :, :ff_cols]),
        side_by_side(pre_all[:, :, ff_cols:]),
        side_by_side(down_all),
    )


def solution(mesh):
    return jax.shard_map(
        on_device,
        mesh=mesh,
        in_specs=(
            P("rep", "fsdp", None),
            P("rep", "fsdp", None),
            P("rep", None),
            P("rep", None),
            P("fsdp"),
            P("fsdp"),
            P("fsdp"),
            P("fsdp"),
            P("fsdp", None),
            P("fsdp", None),
            P("fsdp", None),
            P("fsdp", None),
            P("fsdp", None),
            P("fsdp", None),
        ),
        out_specs=(
            P("rep", "fsdp", None),
            P("rep", "fsdp", None),
            P("fsdp"),
            P("fsdp"),
            P("fsdp"),
            P("fsdp"),
            P("fsdp", None),
            P("fsdp", None),
            P("fsdp", None),
            P("fsdp", None),
            P("fsdp", None),
            P("fsdp", None),
        ),
        check_vma=False,
    )
```

time: 4060 us -> 1000 us (0.25)
  waiting for transfers between devices: 3470 us -> 629 us
  matrix products: 237 us -> 89.2 us
  blocking collectives: 92.2 us -> 0 us
  other arithmetic: 170 us -> 94 us
  local copies, waits for them, and re-layouts: 64.8 us -> 136 us
    all_gather x11 -> x6, waiting for transfers between devices: 1900 us -> 128 us  [the longest x3 101 us: all_columns(): lax.all_gather(owned, 'rep', axis=0, axis_index_groups=plane_groups())]
    reduce_scatter x2 -> x3, waiting for transfers between devices: 1480 us -> 102 us  [sum_owned(): lax.psum_scatter(partial.astype(jnp.bfloat16), 'fsdp', scatter_dimension=...]
    ppermute x0 -> x26, waiting for transfers between devices: none -> 268 us  [the longest x24 256 us: exchange(): return lax.ppermute(value, 'rep', [(i, i ^ bit) for i in range(count)])]
    concatenate x2 -> x16, other arithmetic: 134 us -> 21.2 us  [the longest x8 9.45 us: plane_gather(): rows = jnp.concatenate([rows, exchange(rows, bit)], axis=0)]
    dot_general x6 -> x4, matrix products: 108 us -> 25.9 us  [contract_rows(): lax.dot_general(left, right, (((0,), (0,)), ((), ())), preferred_element_...]
    convert_element_type x0 -> x10, local copies, waits for them, and re-layouts: none -> 52.6 us  [the longest x8 48.1 us: side_by_side(): blocks.transpose(1, 0, 2).reshape(rows, lanes * columns).astype(jnp.float32)]
    psum x1, waiting for transfers between devices: 83.2 us -> 129 us  [on_device(): small = lax.psum(small, ('fsdp', 'rep'))]
    dot_general x6 -> x4, matrix products: 63.4 us -> 20.2 us  [contract_cols(): lax.dot_general(left, right, (((1,), (1,)), ((), ())), preferred_element_...]
  transfers between devices with their start and end apart: 14 -> 36, of which waited for: 13 -> 27; matrix products, arithmetic and copies ran while one was open for 8% -> 24% of each run, Pallas kernels for 0% -> 0%
where the time goes in v1:
time: 1000 us; the launch traced here: 996 us
  waiting for transfers between devices  629 us (63%)
  local copies, waits for them, and re-layouts  136 us (14%)
  other arithmetic  94 us (9%)
  matrix products  89.2 us (9%)
  starting transfers between devices  31.6 us (3%)
  between operations  15.8 us (2%)
    ppermute x24, waiting for transfers between devices, exchange(): return lax.ppermute(value, 'rep', [(i, i ^ bit) for i in range(count)])  256 us
    psum x1, waiting for transfers between devices, on_device(): small = lax.psum(small, ('fsdp', 'rep'))  129 us
    reduce_scatter x3, waiting for transfers between devices, sum_owned(): lax.psum_scatter(partial.astype(jnp.bfloat16), 'fsdp', scatter_dimension=...  102 us
    all_gather x3, waiting for transfers between devices, all_columns(): lax.all_gather(owned, 'rep', axis=0, axis_index_groups=plane_groups())  101 us
    convert_element_type x8, local copies, waits for them, and re-layouts, side_by_side(): blocks.transpose(1, 0, 2).reshape(rows, lanes * columns).astype(jnp.float32)  48.1 us
    unnamed x148, local copies, waits for them, and re-layouts  41.3 us
    dot_general x4, matrix products, matmul(): return jnp.dot(left, right, preferred_element_type=jnp.float32)  29.8 us
    ppermute x24, starting transfers between devices, exchange(): return lax.ppermute(value, 'rep', [(i, i ^ bit) for i in range(count)])  26.4 us
  transfers between devices with their start and end apart: 36, of which 27 were waited for; matrix products, arithmetic and copies ran while one was open for 24% of the time, Pallas kernels for 0%

profile of v1, /device:TPU:0, one launch (start us, length us, event | category | flops | bytes accessed | tf_op | source)
XLA Modules:
  0.0 995.6 jit_solution(17202461867038339687)
XLA Ops:
  20.0 12.6 %collective-permute-done = bf16[128,2176]{1,0:T(8,128)(2,1)S(1)} collective-permute-done((bf16[128,2176]{1,0:T(8,128)(2,1)S(1)}, bf16[128,2176]{1,0:T(8,128)(2,1)S(1)}, u32[]{:S(2)}, u32[]{:S(2)}) %collective-permute-start) | collective-permute-done | bytes 557088 | tf_op jit(solution)/shard_map/ppermute | solution.py:70
  34.5 24.1 %collective-permute-done.1 = bf16[256,2176]{1,0:T(8,128)(2,1)S(1)} collective-permute-done((bf16[256,2176]{1,0:T(8,128)(2,1)S(1)}, bf16[256,2176]{1,0:T(8,128)(2,1)S(1)}, u32[]{:S(2)}, u32[]{:S(2)}) %collective-permute-start.1) | collective-permute-done | bytes 1114144 | tf_op jit(solution)/shard_map/ppermute | solution.py:70
  74.2 15.9 %all-gather.10.cloned.1.call-done = bf16[2048,896]{1,0:T(8,128)(2,1)} async-done(((bf16[512,896]{1,0:T(8,128)(2,1)}), bf16[2048,896]{1,0:T(8,128)(2,1)}) %all-gather.10.cloned.1.call-update) | async-done | bytes 3670032 | tf_op jit(solution)/shard_map/all_gather | solution.py:174
  144.4 23.7 %collective-permute-done.5 = bf16[256,2048]{1,0:T(8,128)(2,1)S(1)} collective-permute-done((bf16[256,2048]{1,0:T(8,128)(2,1)S(1)}, bf16[256,2048]{1,0:T(8,128)(2,1)S(1)}, u32[]{:S(2)}, u32[]{:S(2)}) %collective-permute-start.5) | collective-permute-done | bytes 1048608 | tf_op jit(solution)/shard_map/ppermute | solution.py:70
  170.1 11.8 %collective-permute-done.6 = bf16[128,2048]{1,0:T(8,128)(2,1)S(1)} collective-permute-done((bf16[128,2048]{1,0:T(8,128)(2,1)S(1)}, bf16[128,2048]{1,0:T(8,128)(2,1)S(1)}, u32[]{:S(2)}, u32[]{:S(2)}) %collective-permute-start.6) | collective-permute-done | bytes 524320 | tf_op jit(solution)/shard_map/ppermute | solution.py:70
  185.5 11.0 %collective-permute-done.7 = bf16[128,2048]{1,0:T(8,128)(2,1)S(1)} collective-permute-done((bf16[128,2048]{1,0:T(8,128)(2,1)S(1)}, bf16[128,2048]{1,0:T(8,128)(2,1)S(1)}, u32[]{:S(2)}, u32[]{:S(2)}) %collective-permute-start.7) | collective-permute-done | bytes 524320 | tf_op jit(solution)/shard_map/ppermute | solution.py:70
  203.0 17.9 %collective-permute-done.8 = bf16[256,2048]{1,0:T(8,128)(2,1)} collective-permute-done((bf16[256,2048]{1,0:T(8,128)(2,1)}, bf16[256,2048]{1,0:T(8,128)(2,1)}, u32[]{:S(2)}, u32[]{:S(2)}) %collective-permute-start.8) | collective-permute-done | bytes 1048608 | tf_op jit(solution)/shard_map/ppermute | solution.py:70
  225.7 24.0 %collective-permute-done.14 = bf16[256,2048]{1,0:T(8,128)(2,1)S(1)} collective-permute-done((bf16[256,2048]{1,0:T(8,128)(2,1)S(1)}, bf16[256,2048]{1,0:T(8,128)(2,1)S(1)}, u32[]{:S(2)}, u32[]{:S(2)}) %collective-permute-start.14) | collective-permute-done | bytes 1048608 | tf_op jit(solution)/shard_map/ppermute | solution.py:70
  251.4 11.6 %fusion.45 = f32[1024,1536]{1,0:T(8,128)} fusion(bf16[2048,1536]{1,0:T(8,128)(2,1)} %all-gather.12.cloned.1.call-done, bf16[512,2048]{1,0:T(8,128)(2,1)} %collective-permute-done.9, bf16[256,2048]{1,0:T(8,128)(2,1)} %collective-permute-done.8, bf16[128,2048]{1,0:T(8,128)(2,1)} %copy-done.39, bf16[128,2048]{1,0:T(8,128)(2,1)} %copy-done.24), kind=kOutput, calls=%fused_computation.138 | convolution fusion | flops 6459228160 | bytes 16777216 | tf_op jit(solution)/shard_map/dot_general | solution.py:17
  263.0 11.8 %all-gather.14.cloned.1.call-done = bf16[2048,768]{1,0:T(8,128)(2,1)} async-done(((bf16[512,768]{1,0:T(8,128)(2,1)}), bf16[2048,768]{1,0:T(8,128)(2,1)}) %all-gather.14.cloned.1.call-update) | async-done | bytes 3145744 | tf_op jit(solution)/shard_map/all_gather | solution.py:184
  274.8 9.2 multiply_convert_fusion.1
  285.2 9.0 fusion.10
  306.7 20.4 %collective-permute-done.17 = bf16[256,2048]{1,0:T(8,128)(2,1)S(1)} collective-permute-done((bf16[256,2048]{1,0:T(8,128)(2,1)S(1)}, bf16[256,2048]{1,0:T(8,128)(2,1)S(1)}, u32[]{:S(2)}, u32[]{:S(2)}) %collective-permute-start.17) | collective-permute-done | bytes 1048608 | tf_op jit(solution)/shard_map/ppermute | solution.py:70
  329.0 20.1 %collective-permute-done.11 = bf16[256,2048]{1,0:T(8,128)(2,1)S(1)} collective-permute-done((bf16[256,2048]{1,0:T(8,128)(2,1)S(1)}, bf16[256,2048]{1,0:T(8,128)(2,1)S(1)}, u32[]{:S(2)}, u32[]{:S(2)}) %collective-permute-start.11) | collective-permute-done | bytes 1048608 | tf_op jit(solution)/shard_map/ppermute | solution.py:70
  351.4 11.6 %collective-permute-done.12 = bf16[128,2048]{1,0:T(8,128)(2,1)S(1)} collective-permute-done((bf16[128,2048]{1,0:T(8,128)(2,1)S(1)}, bf16[128,2048]{1,0:T(8,128)(2,1)S(1)}, u32[]{:S(2)}, u32[]{:S(2)}) %collective-permute-start.12) | collective-permute-done | bytes 524320 | tf_op jit(solution)/shard_map/ppermute | solution.py:70
  366.3 11.1 %collective-permute-done.19 = bf16[128,2048]{1,0:T(8,128)(2,1)S(1)} collective-permute-done((bf16[128,2048]{1,0:T(8,128)(2,1)S(1)}, bf16[128,2048]{1,0:T(8,128)(2,1)S(1)}, u32[]{:S(2)}, u32[]{:S(2)}) %collective-permute-start.19) | collective-permute-done | bytes 524320 | tf_op jit(solution)/shard_map/ppermute | solution.py:70
  379.0 21.5 %collective-permute-done.20 = bf16[256,2048]{1,0:T(8,128)(2,1)S(1)} collective-permute-done((bf16[256,2048]{1,0:T(8,128)(2,1)S(1)}, bf16[256,2048]{1,0:T(8,128)(2,1)S(1)}, u32[]{:S(2)}, u32[]{:S(2)}) %collective-permute-start.20) | collective-permute-done | bytes 1048608 | tf_op jit(solution)/shard_map/ppermute | solution.py:70
  403.4 6.8 convolution_convert_fusion.1
  479.7 10.5 %convolution_convert_fusion = bf16[2048,1536]{1,0:T(8,128)(2,1)} fusion(bf16[1024,768]{1,0:T(8,128)(2,1)} %copy-done.63, bf16[1024,768]{1,0:T(8,128)(2,1)S(1)} %copy-done.62, bf16[512,2048]{1,0:T(8,128)(2,1)} %collective-permute-done.9, bf16[256,2048]{1,0:T(8,128)(2,1)} %collective-permute-done.8, bf16[128,2048]{1,0:T(8,128)(2,1)S(1)} %copy-done.40, ...), kind=kOutput, calls=%fused_computation.9 | convolution fusion | flops 6468665344 | bytes 13631488 | tf_op jit(solution)/shard_map/dot_general | solution.py:21
  505.9 23.7 %collective-permute-done.24 = bf16[256,2048]{1,0:T(8,128)(2,1)} collective-permute-done((bf16[256,2048]{1,0:T(8,128)(2,1)S(1)}, bf16[256,2048]{1,0:T(8,128)(2,1)}, u32[]{:S(2)}, u32[]{:S(2)}) %collective-permute-start.24) | collective-permute-done | bytes 1048608 | tf_op jit(solution)/shard_map/ppermute | solution.py:70
  535.0 10.8 %collective-permute-done.25 = bf16[128,2048]{1,0:T(8,128)(2,1)S(1)} collective-permute-done((bf16[128,2048]{1,0:T(8,128)(2,1)}, bf16[128,2048]{1,0:T(8,128)(2,1)S(1)}, u32[]{:S(2)}, u32[]{:S(2)}) %collective-permute-start.25) | collective-permute-done | bytes 524320 | tf_op jit(solution)/shard_map/ppermute | solution.py:70
  549.4 102.2 %reduce-scatter.6.cloned.1.call-done = bf16[512,1536]{1,0:T(8,128)(2,1)} async-done(((bf16[2048,1536]{1,0:T(8,128)(2,1)}), bf16[512,1536]{1,0:T(8,128)(2,1)}) %reduce-scatter.6.cloned.1.call-update) | async-done | bytes 1572880 | tf_op jit(solution)/shard_map/reduce_scatter | solution.py:95
  654.1 128.8 %all-reduce.9.cloned.1.call-done = f32[24,2048]{1,0:T(8,128)} async-done(((f32[24,2048]{1,0:T(8,128)}), f32[24,2048]{1,0:T(8,128)}) %all-reduce.9.cloned.1.call-update) | async-done | bytes 196624 | tf_op jit(solution)/shard_map/psum | solution.py:363
  788.4 42.7 %all-gather.20.cloned.1.call-done = bf16[4096,768]{1,0:T(8,128)(2,1)} async-done(((bf16[512,768]{1,0:T(8,128)(2,1)}), bf16[4096,768]{1,0:T(8,128)(2,1)}) %all-gather.20.cloned.1.call-update) | async-done | bytes 6291472 | tf_op jit(solution)/shard_map/all_gather | solution.py:108
  831.1 8.7 convert_bitcast_fusion
  839.8 11.7 %copy.135 = f32[8,64,8,768]{3,2,0,1:T(8,128)} copy(f32[8,64,8,768]{3,2,1,0:T(8,128)} %convert_bitcast_fusion) | data formatting | bytes 25165824 | tf_op jit(solution)/shard_map/convert_element_type | solution.py:113
  851.5 28.1 %all-gather.16.cloned.1.call-done = bf16[4096,768]{0,1:T(8,128)(2,1)} async-done(((bf16[512,768]{0,1:T(8,128)(2,1)}), bf16[4096,768]{0,1:T(8,128)(2,1)}) %all-gather.16.cloned.1.call-update) | async-done | bytes 6291472 | tf_op jit(solution)/shard_map/all_gather | solution.py:108
  879.6 7.0 copy.147
  923.6 29.7 %all-gather.18.cloned.1.call-done = bf16[4096,1536]{1,0:T(8,128)(2,1)} async-done(((bf16[512,1536]{1,0:T(8,128)(2,1)}), bf16[4096,1536]{1,0:T(8,128)(2,1)}) %all-gather.18.cloned.1.call-update) | async-done | bytes 12582928 | tf_op jit(solution)/shard_map/all_gather | solution.py:108
  953.3 12.7 %convert_bitcast_fusion.1 = (f32[8,64,8,768]{3,2,1,0:T(8,128)}, f32[8,64,8,768]{3,2,1,0:T(8,128)}) fusion(bf16[8,512,1536]{2,1,0:T(8,128)(2,1)} %bitcast.248), kind=kLoop, calls=%fused_computation.2 | loop fusion | flops 6291456 | bytes 37748736
  966.0 11.2 %copy.133 = f32[8,64,8,768]{3,2,0,1:T(8,128)} copy(f32[8,64,8,768]{3,2,1,0:T(8,128)} %get-tuple-element.32) | data formatting | bytes 25165824 | tf_op jit(solution)/shard_map/convert_element_type | solution.py:113
  977.3 11.2 %copy.134 = f32[8,64,8,768]{3,2,0,1:T(8,128)} copy(f32[8,64,8,768]{3,2,1,0:T(8,128)} %get-tuple-element.31) | data formatting | bytes 25165824 | tf_op jit(solution)/shard_map/convert_element_type | solution.py:113
  (371 shorter events, 266.7 us)
Async XLA Ops:
  7.2 82.9 %all-gather.10.cloned.1.call-start = ((), (), s32[]{:S(2)}) async-start(), calls=%async_computation.3 | async-start | bytes 4587520 | tf_op jit(solution)/shard_map/all_gather | solution.py:174
  15.1 236.3 %all-gather.12.cloned.1.call-start = ((), (), s32[]{:S(2)}) async-start(), calls=%async_computation.4 | async-start | bytes 7864320 | tf_op jit(solution)/shard_map/all_gather | solution.py:175
  16.9 15.7 %collective-permute-start = (bf16[128,2176]{1,0:T(8,128)(2,1)S(1)}, bf16[128,2176]{1,0:T(8,128)(2,1)S(1)}, u32[]{:S(2)}, u32[]{:S(2)}) collective-permute-start(bf16[128,2176]{1,0:T(8,128)(2,1)S(1)} %pad_maximum_fusion.27), channel_id=1, source_target_pairs={{0,2},{1,3},{2,0},{3,1},{4,6},{5,7},{6,4},{7,5},{8,10},{9,11},{10,... | collective-permute-start | bytes 1671176 | tf_op jit(solution)/shard_map/ppermute | solution.py:70
  32.7 25.9 %collective-permute-start.1 = (bf16[256,2176]{1,0:T(8,128)(2,1)S(1)}, bf16[256,2176]{1,0:T(8,128)(2,1)S(1)}, u32[]{:S(2)}, u32[]{:S(2)}) collective-permute-start(bf16[256,2176]{1,0:T(8,128)(2,1)S(1)} %pad_maximum_fusion.16), channel_id=1, source_target_pairs={{0,4},{1,5},{2,6},{3,7},{4,0},{5,1},{6,2},{7,3},{8,12},{9,13},{10,... | collective-permute-start | bytes 3342344 | tf_op jit(solution)/shard_map/ppermute | solution.py:70
  63.0 211.8 %all-gather.14.cloned.1.call-start = ((), (), s32[]{:S(2)}) async-start(), calls=%async_computation.5 | async-start | bytes 3932160 | tf_op jit(solution)/shard_map/all_gather | solution.py:184
  108.3 13.6 %collective-permute-start.3 = (bf16[8,64,256]{2,1,0:T(8,128)(2,1)}, bf16[8,64,256]{2,1,0:T(8,128)(2,1)}, u32[]{:S(2)}, u32[]{:S(2)}) collective-permute-start(bf16[8,64,256]{2,1,0:T(8,128)(2,1)} %pad_maximum_fusion.31), channel_id=1, source_target_pairs={{0,8},{8,16},{16,24},{1,9},{9,17},{17,25},{2,10},{10,18},{18,26},{... | collective-permute-start | bytes 786440 | tf_op jit(solution)/shard_map/ppermute | solution.py:236
  142.9 25.3 %collective-permute-start.5 = (bf16[256,2048]{1,0:T(8,128)(2,1)S(1)}, bf16[256,2048]{1,0:T(8,128)(2,1)S(1)}, u32[]{:S(2)}, u32[]{:S(2)}) collective-permute-start(bf16[256,2048]{1,0:T(8,128)(2,1)S(1)} %slice.492), channel_id=1, source_target_pairs={{0,4},{1,5},{2,6},{3,7},{4,0},{5,1},{6,2},{7,3},{8,12},{9,13},{10,... | collective-permute-start | bytes 3145736 | tf_op jit(solution)/shard_map/ppermute | solution.py:70
  168.6 13.3 %collective-permute-start.6 = (bf16[128,2048]{1,0:T(8,128)(2,1)S(1)}, bf16[128,2048]{1,0:T(8,128)(2,1)S(1)}, u32[]{:S(2)}, u32[]{:S(2)}) collective-permute-start(bf16[128,2048]{1,0:T(8,128)(2,1)S(1)} %slice.496), channel_id=1, source_target_pairs={{0,2},{1,3},{2,0},{3,1},{4,6},{5,7},{6,4},{7,5},{8,10},{9,11},{10,... | collective-permute-start | bytes 1572872 | tf_op jit(solution)/shard_map/ppermute | solution.py:70
  184.0 12.5 %collective-permute-start.7 = (bf16[128,2048]{1,0:T(8,128)(2,1)S(1)}, bf16[128,2048]{1,0:T(8,128)(2,1)S(1)}, u32[]{:S(2)}, u32[]{:S(2)}) collective-permute-start(bf16[128,2048]{1,0:T(8,128)(2,1)S(1)} %multiply_convert_fusion.5), channel_id=1, source_target_pairs={{0,2},{1,3},{2,0},{3,1},{4,6},{5,7},{6,4},{7,5},{8,10},{9,11},{10,... | collective-permute-start | bytes 1572872 | tf_op jit(solution)/shard_map/ppermute | solution.py:70
  197.6 23.3 %collective-permute-start.8 = (bf16[256,2048]{1,0:T(8,128)(2,1)}, bf16[256,2048]{1,0:T(8,128)(2,1)}, u32[]{:S(2)}, u32[]{:S(2)}) collective-permute-start(bf16[256,2048]{1,0:T(8,128)(2,1)} %pad_maximum_fusion.17), channel_id=1, source_target_pairs={{0,4},{1,5},{2,6},{3,7},{4,0},{5,1},{6,2},{7,3},{8,12},{9,13},{10,... | collective-permute-start | bytes 3145736 | tf_op jit(solution)/shard_map/ppermute | solution.py:70
  201.2 346.5 %reduce-scatter.8.cloned.1.call-start = ((), (), s32[]{:S(2)}) async-start(), calls=%async_computation.9 | async-start | bytes 3932160 | tf_op jit(solution)/shard_map/reduce_scatter | solution.py:95
  201.4 22.6 %collective-permute-start.13 = (bf16[128,2048]{1,0:T(8,128)(2,1)}, bf16[128,2048]{1,0:T(8,128)(2,1)S(1)}, u32[]{:S(2)}, u32[]{:S(2)}) collective-permute-start(bf16[128,2048]{1,0:T(8,128)(2,1)} %bitcast.260), channel_id=1, source_target_pairs={{0,2},{1,3},{2,0},{3,1},{4,6},{5,7},{6,4},{7,5},{8,10},{9,11},{10,... | collective-permute-start | bytes 1572872 | tf_op jit(solution)/shard_map/ppermute | solution.py:70
  224.0 27.4 %collective-permute-start.9 = (bf16[512,2048]{1,0:T(8,128)(2,1)}, bf16[512,2048]{1,0:T(8,128)(2,1)}, u32[]{:S(2)}, u32[]{:S(2)}) collective-permute-start(bf16[512,2048]{1,0:T(8,128)(2,1)} %pad_maximum_fusion.10), channel_id=1, source_target_pairs={{0,1},{1,0},{2,3},{3,2},{4,5},{5,4},{6,7},{7,6},{8,9},{9,8},{10,11... | collective-permute-start | bytes 6291464 | tf_op jit(solution)/shard_map/ppermute | solution.py:70
  224.1 25.6 %collective-permute-start.14 = (bf16[256,2048]{1,0:T(8,128)(2,1)S(1)}, bf16[256,2048]{1,0:T(8,128)(2,1)S(1)}, u32[]{:S(2)}, u32[]{:S(2)}) collective-permute-start(bf16[256,2048]{1,0:T(8,128)(2,1)S(1)} %pad_maximum_fusion.18), channel_id=1, source_target_pairs={{0,4},{1,5},{2,6},{3,7},{4,0},{5,1},{6,2},{7,3},{8,12},{9,13},{10,... | collective-permute-start | bytes 3145736 | tf_op jit(solution)/shard_map/ppermute | solution.py:70
  251.4 11.7 %collective-permute-start.15 = (bf16[512,2048]{1,0:T(8,128)(2,1)}, bf16[512,2048]{1,0:T(8,128)(2,1)}, u32[]{:S(2)}, u32[]{:S(2)}) collective-permute-start(bf16[512,2048]{1,0:T(8,128)(2,1)} %pad_maximum_fusion.11), channel_id=1, source_target_pairs={{0,1},{1,0},{2,3},{3,2},{4,5},{5,4},{6,7},{7,6},{8,9},{9,8},{10,11... | collective-permute-start | bytes 6291464 | tf_op jit(solution)/shard_map/ppermute | solution.py:70
  294.6 5.4 collective-permute-start.16
  301.0 26.1 %collective-permute-start.17 = (bf16[256,2048]{1,0:T(8,128)(2,1)S(1)}, bf16[256,2048]{1,0:T(8,128)(2,1)S(1)}, u32[]{:S(2)}, u32[]{:S(2)}) collective-permute-start(bf16[256,2048]{1,0:T(8,128)(2,1)S(1)} %slice.490), channel_id=1, source_target_pairs={{0,4},{1,5},{2,6},{3,7},{4,0},{5,1},{6,2},{7,3},{8,12},{9,13},{10,... | collective-permute-start | bytes 3145736 | tf_op jit(solution)/shard_map/ppermute | solution.py:70
  305.1 44.0 %collective-permute-start.11 = (bf16[256,2048]{1,0:T(8,128)(2,1)S(1)}, bf16[256,2048]{1,0:T(8,128)(2,1)S(1)}, u32[]{:S(2)}, u32[]{:S(2)}) collective-permute-start(bf16[256,2048]{1,0:T(8,128)(2,1)S(1)} %slice.491), channel_id=1, source_target_pairs={{0,4},{1,5},{2,6},{3,7},{4,0},{5,1},{6,2},{7,3},{8,12},{9,13},{10,... | collective-permute-start | bytes 3145736 | tf_op jit(solution)/shard_map/ppermute | solution.py:70
  327.4 23.6 %collective-permute-start.18 = (bf16[128,2048]{1,0:T(8,128)(2,1)S(1)}, bf16[128,2048]{1,0:T(8,128)(2,1)S(1)}, u32[]{:S(2)}, u32[]{:S(2)}) collective-permute-start(bf16[128,2048]{1,0:T(8,128)(2,1)S(1)} %slice.494), channel_id=1, source_target_pairs={{0,2},{1,3},{2,0},{3,1},{4,6},{5,7},{6,4},{7,5},{8,10},{9,11},{10,... | collective-permute-start | bytes 1572872 | tf_op jit(solution)/shard_map/ppermute | solution.py:70
  349.5 13.5 %collective-permute-start.12 = (bf16[128,2048]{1,0:T(8,128)(2,1)S(1)}, bf16[128,2048]{1,0:T(8,128)(2,1)S(1)}, u32[]{:S(2)}, u32[]{:S(2)}) collective-permute-start(bf16[128,2048]{1,0:T(8,128)(2,1)S(1)} %slice.495), channel_id=1, source_target_pairs={{0,2},{1,3},{2,0},{3,1},{4,6},{5,7},{6,4},{7,5},{8,10},{9,11},{10,... | collective-permute-start | bytes 1572872 | tf_op jit(solution)/shard_map/ppermute | solution.py:70
  364.8 12.6 %collective-permute-start.19 = (bf16[128,2048]{1,0:T(8,128)(2,1)S(1)}, bf16[128,2048]{1,0:T(8,128)(2,1)S(1)}, u32[]{:S(2)}, u32[]{:S(2)}) collective-permute-start(bf16[128,2048]{1,0:T(8,128)(2,1)S(1)} %get-tuple-element.25), channel_id=1, source_target_pairs={{0,2},{1,3},{2,0},{3,1},{4,6},{5,7},{6,4},{7,5},{8,10},{9,11},{10,... | collective-permute-start | bytes 1572872 | tf_op jit(solution)/shard_map/ppermute | solution.py:70
  377.5 23.1 %collective-permute-start.20 = (bf16[256,2048]{1,0:T(8,128)(2,1)S(1)}, bf16[256,2048]{1,0:T(8,128)(2,1)S(1)}, u32[]{:S(2)}, u32[]{:S(2)}) collective-permute-start(bf16[256,2048]{1,0:T(8,128)(2,1)S(1)} %pad_maximum_fusion.19), channel_id=1, source_target_pairs={{0,4},{1,5},{2,6},{3,7},{4,0},{5,1},{6,2},{7,3},{8,12},{9,13},{10,... | collective-permute-start | bytes 3145736 | tf_op jit(solution)/shard_map/ppermute | solution.py:70
  402.2 8.5 collective-permute-start.21
  410.2 138.2 %reduce-scatter.4.cloned.1.call-start = ((), (), s32[]{:S(2)}) async-start(), calls=%async_computation.7 | async-start | bytes 3932160 | tf_op jit(solution)/shard_map/reduce_scatter | solution.py:95
  429.3 23.1 %collective-permute-start.22 = (bf16[8,64,256]{2,1,0:T(8,128)(2,1)}, bf16[8,64,256]{2,1,0:T(8,128)(2,1)}, u32[]{:S(2)}, u32[]{:S(2)}) collective-permute-start(bf16[8,64,256]{2,1,0:T(8,128)(2,1)} %fusion.53), channel_id=1, source_target_pairs={{8,0},{16,8},{24,16},{9,1},{17,9},{25,17},{10,2},{18,10},{26,18},{... | collective-permute-start | bytes 786440 | tf_op jit(solution)/shard_map/ppermute | solution.py:315
  478.0 173.6 %reduce-scatter.6.cloned.1.call-start = ((), (), s32[]{:S(2)}) async-start(), calls=%async_computation.8 | async-start | bytes 7864320 | tf_op jit(solution)/shard_map/reduce_scatter | solution.py:95
  490.2 292.6 %all-reduce.9.cloned.1.call-start = ((), (), s32[]{:S(2)}) async-start(), calls=%async_computation.6 | async-start | bytes 393216 | tf_op jit(solution)/shard_map/psum | solution.py:363
  504.2 25.4 %collective-permute-start.24 = (bf16[256,2048]{1,0:T(8,128)(2,1)S(1)}, bf16[256,2048]{1,0:T(8,128)(2,1)}, u32[]{:S(2)}, u32[]{:S(2)}) collective-permute-start(bf16[256,2048]{1,0:T(8,128)(2,1)S(1)} %slice.489), channel_id=1, source_target_pairs={{0,4},{1,5},{2,6},{3,7},{4,0},{5,1},{6,2},{7,3},{8,12},{9,13},{10,... | collective-permute-start | bytes 3145736 | tf_op jit(solution)/shard_map/ppermute | solution.py:70
  532.5 13.3 %collective-permute-start.25 = (bf16[128,2048]{1,0:T(8,128)(2,1)}, bf16[128,2048]{1,0:T(8,128)(2,1)S(1)}, u32[]{:S(2)}, u32[]{:S(2)}) collective-permute-start(bf16[128,2048]{1,0:T(8,128)(2,1)} %slice.493), channel_id=1, source_target_pairs={{0,2},{1,3},{2,0},{3,1},{4,6},{5,7},{6,4},{7,5},{8,10},{9,11},{10,... | collective-permute-start | bytes 1572872 | tf_op jit(solution)/shard_map/ppermute | solution.py:70
  547.6 283.5 %all-gather.20.cloned.1.call-start = ((), (), s32[]{:S(2)}) async-start(), calls=%async_computation.12 | async-start | bytes 7077888 | tf_op jit(solution)/shard_map/all_gather | solution.py:108
  548.4 331.2 %all-gather.16.cloned.1.call-start = ((), (), s32[]{:S(2)}) async-start(), calls=%async_computation.10 | async-start | bytes 7077888 | tf_op jit(solution)/shard_map/all_gather | solution.py:108
  549.1 404.2 %all-gather.18.cloned.1.call-start = ((), (), s32[]{:S(2)}) async-start(), calls=%async_computation.11 | async-start | bytes 14155776 | tf_op jit(solution)/shard_map/all_gather | solution.py:108
  (68 other events, 484.8 us)
Sparse Core Ops, SparseCore 0:
  15.2 74.8 all-gather.9
  92.2 115.3 all-gather.11
  209.2 65.5 all-gather.13
  410.3 64.6 reduce-scatter.7
  478.1 59.9 reduce-scatter.3
  540.9 110.6 reduce-scatter.5
  657.7 125.1 all-reduce.8
  784.7 46.3 all-gather.19
  833.0 46.5 all-gather.15
  881.3 71.9 all-gather.17
